TPU v7x, 32 devices: a whole 2x2x4 slice. The times are simulated.
32 devices in a mesh: station: 8 (over y, x, core), tm: 4 (over z).
Axes of the slice: x: 2, y: 2, z: 4, core: 2. Of those that a mesh axis runs over, the one named last changes fastest.
Arguments:
- samples: bfloat16 [64, 256, 2048], P('tm', 'station'), may hold values from -6 to 6
- history: bfloat16 [15, 256, 2048], P(None, 'station'), may hold values from -6 to 6
- taps: float32 [16, 2048], replicated, may hold values from -0.03125 to 0.03125
Outputs:
- visibility: float32 [1024, 2, 256, 256], P(('station', 'tm'))
- beam_power: float32 [64, 1024], P('tm', 'station')
All inputs are finite; a program needn't handle non-finite values.
Results may differ from a plain program's by a relative error of at most 0.0095.
Values may be sent and summed in bfloat16 or wider, within the bound.
A program may use at most 128 MiB of HBM per device.

v0:
```python
import math
import jax
import jax.numpy as jnp
from jax import lax
from jax.sharding import PartitionSpec as P


def passed_along(block, axis, distance):
    devices = range(lax.axis_size(axis))
    route = [(i - distance, i) for i in devices if i - distance in devices]
    return lax.ppermute(block, axis, route)


def dft_parts(frame_len, channels):
    sample_index = jnp.arange(frame_len, dtype=jnp.int32)
    channel_index = jnp.arange(channels, dtype=jnp.int32)
    phases = sample_index[:, None] * channel_index[None, :] % frame_len
    angles = phases.astype(jnp.float32) * (2.0 * math.pi / frame_len)
    return (jnp.cos(angles).astype(jnp.bfloat16), (-jnp.sin(angles)).astype(jnp.bfloat16))


def filter_frames(extended, taps, frames_out):
    span_taps = taps.shape[0]
    running = jnp.zeros((frames_out,) + extended.shape[1:], jnp.float32)
    for tap_index in range(span_taps):
        offset = span_taps - 1 - tap_index
        running = running + taps[tap_index][None, None, :] * extended[
            offset : offset + frames_out
        ].astype(jnp.float32)
    return jnp.swapaxes(running, 0, 1).astype(jnp.bfloat16)


def power_of(grouped):
    values = grouped.astype(jnp.float32)
    return jnp.sum(values * values, axis=(-3, -2)) * (1.0 / grouped.shape[-3])


def flat_pair(piece):
    chan_count, input_count, pair_count, frame_count = piece.shape
    flat = piece.reshape(chan_count, input_count, pair_count * frame_count)
    rotated = jnp.concatenate([-piece[:, :, 1:2], piece[:, :, 0:1]], axis=2)
    return (flat, rotated.reshape(chan_count, input_count, pair_count * frame_count))


def correlate(piece, norm_scale):
    flat, rotated = flat_pair(piece)
    real_part = (
        jnp.einsum("cak,cbk->cab", flat, flat, preferred_element_type=jnp.float32) * norm_scale
    )
    imag_part = (
        jnp.einsum("cak,cbk->cab", rotated, flat, preferred_element_type=jnp.float32) * norm_scale
    )
    return (real_part, imag_part)


def body(samples, history, taps):
    frames_dev = samples.shape[0]
    frame_len = samples.shape[2]
    span_taps = taps.shape[0]
    cos_part, sin_part = dft_parts(frame_len, frame_len // 2)
    tail_block = samples[frames_dev - (span_taps - 1) :]
    prior_frames = passed_along(tail_block, "tm", 1)
    prior_frames = jnp.where(lax.axis_index("tm") == 0, history, prior_frames)
    extended = jnp.concatenate([prior_frames, samples], axis=0)
    weighted = filter_frames(extended, taps, frames_dev)
    real_spec = jnp.einsum("nc,atn->cat", cos_part, weighted, preferred_element_type=jnp.float32)
    imag_spec = jnp.einsum("nc,atn->cat", sin_part, weighted, preferred_element_type=jnp.float32)
    spectra = jnp.stack([real_spec, imag_spec], axis=2).astype(jnp.bfloat16)
    time_groups = lax.axis_size("tm")
    norm_scale = 1.0 / (frames_dev * time_groups)
    gathered = lax.all_to_all(
        lax.all_to_all(spectra[None], "station", split_axis=1, concat_axis=2, tiled=True),
        "tm",
        split_axis=1,
        concat_axis=0,
        tiled=True,
    )
    own_channels = gathered.shape[1]
    inputs = gathered.shape[2]
    power_own = power_of(gathered)
    power_back = lax.all_to_all(power_own, "tm", split_axis=0, concat_axis=1, tiled=True)
    power_rows = jnp.transpose(power_back[0])

    def accumulate(block_index, running):
        time_piece = lax.dynamic_index_in_dim(gathered, block_index, 0, keepdims=False)
        real_part, imag_part = correlate(time_piece, norm_scale)
        partial_value = jnp.stack([real_part, imag_part], axis=1).astype(jnp.bfloat16)
        partial_value = lax.optimization_barrier(partial_value)
        return running + partial_value.astype(jnp.float32)

    initial_sum = jnp.zeros((own_channels, 2, inputs, inputs), jnp.float32)
    visibility = lax.fori_loop(0, time_groups, accumulate, initial_sum)
    return (visibility, power_rows)


def solution(mesh):
    return jax.shard_map(
        body,
        mesh=mesh,
        in_specs=(P("tm", "station", None), P(None, "station", None), P()),
        out_specs=(P(("station", "tm"), None, None, None), P("tm", "station")),
        check_vma=False,
    )
```

profile of v0, /device:TPU:0, one launch (start us, length us, event | category | flops | bytes accessed | tf_op | source)
XLA Modules:
  0.0 371.6 jit_solution(146463902237839219)
XLA Ops:
  3.8 6.2 %collective-permute-start = (bf16[15,32,2048]{2,1,0:T(8,128)(2,1)}, bf16[15,32,2048]{2,1,0:T(8,128)(2,1)}, u32[]{:S(2)}, u32[]{:S(2)}) collective-permute-start(bf16[15,32,2048]{2,1,0:T(8,128)(2,1)} %slice.112), channel_id=1, source_target_pairs={{0,1},{1,2},{2,3},{4,5},{5,6},{6,7},{8,9},{9,10},{10,11},{12,13},{... | collective-permute-start | bytes 5898248 | tf_op jit(solution)/shard_map/ppermute | solution.py:11
  11.7 39.5 %collective-permute-done = bf16[15,32,2048]{2,1,0:T(8,128)(2,1)} collective-permute-done((bf16[15,32,2048]{2,1,0:T(8,128)(2,1)}, bf16[15,32,2048]{2,1,0:T(8,128)(2,1)}, u32[]{:S(2)}, u32[]{:S(2)}) %collective-permute-start) | collective-permute-done | bytes 1966112 | tf_op jit(solution)/shard_map/ppermute | solution.py:11
  52.9 9.5 %add_convert_fusion = bf16[16,32,2048]{2,1,0:T(8,128)(2,1)S(1)} fusion(bf16[16,32,2048]{2,1,0:T(8,128)(2,1)S(1)} %copy-done, bf16[15,32,2048]{2,1,0:T(8,128)(2,1)S(1)} %broadcast_select_fusion, f32[2048]{0:T(1024)S(1)} %bitcast.116, f32[2048]{0:T(1024)S(1)} %bitcast.117, f32[2048]{0:T(1024)S(1)} %bitcast.103, f32[2048]{0:T(1024)S(1)} %bitcast.104, ...), kind=kLoop, calls=%fused_computation.53 | loop fusion | flops 66060288 | bytes 6291456 | tf_op jit(solution)/shard_map/convert_element_type | solution.py:30
  62.4 31.8 %fusion.42 = bf16[1,1024,32,1,16]{1,2,4,3,0:T(8,128)(2,1)S(1)} fusion(bf16[16,32,2048]{2,1,0:T(8,128)(2,1)S(1)} %add_convert_fusion), kind=kOutput, calls=%fused_computation.75 | convolution fusion | flops 2179465216 | bytes 3145728 | tf_op jit(solution)/shard_map/nc,atn->cat/dot_general | solution.py:66
  94.2 32.5 %fusion.47 = bf16[1,1024,32,1,16]{1,2,4,3,0:T(8,128)(2,1)S(1)} fusion(bf16[16,32,2048]{2,1,0:T(8,128)(2,1)S(1)} %add_convert_fusion), kind=kOutput, calls=%fused_computation.76 | convolution fusion | flops 2181562368 | bytes 3145728 | tf_op jit(solution)/shard_map/nc,atn->cat/dot_general | solution.py:67
  126.8 12.1 %copy.33 = bf16[1,1024,32,2,16]{2,4,3,0,1:T(8,128)(2,1)} copy(bf16[1,1024,32,2,16]{1,2,4,3,0:T(8,128)(2,1)S(1)} %pad_maximum_fusion.3) | data formatting | bytes 4194304 | tf_op jit(solution)/shard_map/stack | solution.py:68
  138.9 10.1 %reshape.82 = bf16[8,2,65536]{2,1,0:T(2,128)(2,1)S(1)} reshape(bf16[1024,1,2,16,32]{4,3,2,1,0:T(8,128)(2,1)} %bitcast.96) | data formatting | bytes 4194304
  149.1 30.2 %all_to_all.39 = bf16[8,2,65536]{2,1,0:T(2,128)(2,1)} all-to-all(bf16[8,2,65536]{2,1,0:T(2,128)(2,1)S(1)} %reshape.82), channel_id=1, replica_groups=mesh['station'=8,'tm'=4] {'station'}, dimensions={0} | all-to-all | bytes 4194304 | tf_op jit(solution)/shard_map/all_to_all | solution.py:72
  179.3 8.6 %reshape.83 = bf16[1024,1,2,16,32]{4,3,2,1,0:T(8,128)(2,1)} reshape(bf16[8,2,65536]{2,1,0:T(2,128)(2,1)} %all_to_all.39) | data formatting | bytes 4194304
  187.9 9.3 %copy.42 = bf16[1,8,128,32,2,16]{2,1,5,4,3,0:T(8,128)(2,1)S(1)} copy(bf16[1,8,128,32,2,16]{3,5,4,2,1,0:T(8,128)(2,1)} %bitcast.97) | data formatting | bytes 4194304 | tf_op jit(solution)/shard_map/all_to_all | solution.py:72
  198.9 4.9 %copy.36 = bf16[1,128,256,2,16]{2,4,3,0,1:T(8,128)(2,1)} copy(bf16[1,128,256,2,16]{1,4,3,2,0:T(8,128)(2,1)} %bitcast.99) | data formatting | bytes 4194304 | tf_op jit(solution)/shard_map/all_to_all | solution.py:72
  203.8 5.8 %all-to-all-start.1 = ((bf16[1,128,256,2,16]{2,4,3,0,1:T(8,128)(2,1)}), bf16[1,128,256,2,16]{2,4,3,0,1:T(8,128)(2,1)S(1)}, u32[]{:S(2)}, u32[]{:S(2)}) async-start(bf16[1,128,256,2,16]{2,4,3,0,1:T(8,128)(2,1)} %copy.36), calls=%async_computation.1 | async-start | bytes 4194304 | tf_op jit(solution)/shard_map/all_to_all | solution.py:71
  209.6 47.5 %all-to-all-done.1 = bf16[1,128,256,2,16]{2,4,3,0,1:T(8,128)(2,1)S(1)} async-done(((bf16[1,128,256,2,16]{2,4,3,0,1:T(8,128)(2,1)}), bf16[1,128,256,2,16]{2,4,3,0,1:T(8,128)(2,1)S(1)}, u32[]{:S(2)}, u32[]{:S(2)}) %all-to-all-start.1) | async-done | bytes 2097184 | tf_op jit(solution)/shard_map/all_to_all | solution.py:71
  258.4 3.2 all-to-all-start.2
  261.7 96.2 %while.14 = (s32[]{:T(128)}, f32[32,2,256,256]{3,2,0,1:T(8,128)}, bf16[4,32,256,2,16]{2,4,3,1,0:T(8,128)(2,1)S(1)}, s32[]{:T(128)}, s32[]{:T(128)}) while((s32[]{:T(128)}, f32[32,2,256,256]{3,2,0,1:T(8,128)}, bf16[4,32,256,2,16]{2,4,3,1,0:T(8,128)(2,1)S(1)}, s32[]{:T(128)}, s32[]{:T(128)}) %tuple.65), condition=%wide.region_1.2_spmd.clone, body=%wide.region_0.1_spmd.clone.sunk | while | flops 293994496 | bytes 72876112 | solution.py:92
  266.4 6.3 %pad_maximum_fusion.7 = bf16[32,2,256,256]{3,2,0,1:T(8,128)(2,1)} fusion(bf16[32,1,256,256]{3,2,0,1:T(8,128)(2,1)S(1)} %fusion.78, bf16[32,1,256,256]{3,2,0,1:T(8,128)(2,1)} %fusion.79), kind=kLoop, calls=%fused_computation.1.clone.1 | loop fusion | flops 4194304 | bytes 16777216 | tf_op jit(solution)/shard_map/while/body/eval_jaxpr/stack | solution.py:87
  272.8 9.9 %select_add_fusion.2 = f32[32,2,256,256]{3,2,0,1:T(8,128)} fusion(f32[32,2,256,256]{3,2,0,1:T(8,128)} %get-tuple-element.149, bf16[32,2,256,256]{3,2,0,1:T(8,128)(2,1)} %pad_maximum_fusion.7, pred[]{:T(512)S(6)} %compare.4), kind=kLoop, calls=%fused_computation.clone.1 | loop fusion | flops 12582912 | bytes 41943040 | tf_op jit(solution)/shard_map/while/body/eval_jaxpr/add | solution.py:89
  287.5 6.3 %pad_maximum_fusion.7 = bf16[32,2,256,256]{3,2,0,1:T(8,128)(2,1)} fusion(bf16[32,1,256,256]{3,2,0,1:T(8,128)(2,1)S(1)} %fusion.78, bf16[32,1,256,256]{3,2,0,1:T(8,128)(2,1)} %fusion.79), kind=kLoop, calls=%fused_computation.1.clone.1 | loop fusion | flops 4194304 | bytes 16777216 | tf_op jit(solution)/shard_map/while/body/eval_jaxpr/stack | solution.py:87
  293.8 14.0 %select_add_fusion.2 = f32[32,2,256,256]{3,2,0,1:T(8,128)} fusion(f32[32,2,256,256]{3,2,0,1:T(8,128)} %get-tuple-element.149, bf16[32,2,256,256]{3,2,0,1:T(8,128)(2,1)} %pad_maximum_fusion.7, pred[]{:T(512)S(6)} %compare.4), kind=kLoop, calls=%fused_computation.clone.1 | loop fusion | flops 12582912 | bytes 41943040 | tf_op jit(solution)/shard_map/while/body/eval_jaxpr/add | solution.py:89
  312.5 6.3 %pad_maximum_fusion.7 = bf16[32,2,256,256]{3,2,0,1:T(8,128)(2,1)} fusion(bf16[32,1,256,256]{3,2,0,1:T(8,128)(2,1)S(1)} %fusion.78, bf16[32,1,256,256]{3,2,0,1:T(8,128)(2,1)} %fusion.79), kind=kLoop, calls=%fused_computation.1.clone.1 | loop fusion | flops 4194304 | bytes 16777216 | tf_op jit(solution)/shard_map/while/body/eval_jaxpr/stack | solution.py:87
  318.9 14.0 %select_add_fusion.2 = f32[32,2,256,256]{3,2,0,1:T(8,128)} fusion(f32[32,2,256,256]{3,2,0,1:T(8,128)} %get-tuple-element.149, bf16[32,2,256,256]{3,2,0,1:T(8,128)(2,1)} %pad_maximum_fusion.7, pred[]{:T(512)S(6)} %compare.4), kind=kLoop, calls=%fused_computation.clone.1 | loop fusion | flops 12582912 | bytes 41943040 | tf_op jit(solution)/shard_map/while/body/eval_jaxpr/add | solution.py:89
  337.6 6.3 %pad_maximum_fusion.7 = bf16[32,2,256,256]{3,2,0,1:T(8,128)(2,1)} fusion(bf16[32,1,256,256]{3,2,0,1:T(8,128)(2,1)S(1)} %fusion.78, bf16[32,1,256,256]{3,2,0,1:T(8,128)(2,1)} %fusion.79), kind=kLoop, calls=%fused_computation.1.clone.1 | loop fusion | flops 4194304 | bytes 16777216 | tf_op jit(solution)/shard_map/while/body/eval_jaxpr/stack | solution.py:87
  343.9 14.0 %select_add_fusion.2 = f32[32,2,256,256]{3,2,0,1:T(8,128)} fusion(f32[32,2,256,256]{3,2,0,1:T(8,128)} %get-tuple-element.149, bf16[32,2,256,256]{3,2,0,1:T(8,128)(2,1)} %pad_maximum_fusion.7, pred[]{:T(512)S(6)} %compare.4), kind=kLoop, calls=%fused_computation.clone.1 | loop fusion | flops 12582912 | bytes 41943040 | tf_op jit(solution)/shard_map/while/body/eval_jaxpr/add | solution.py:89
  357.9 11.7 %copy.41 = f32[32,2,256,256]{3,2,1,0:T(8,128)} copy(f32[32,2,256,256]{3,2,0,1:T(8,128)} %get-tuple-element.94) | data formatting | bytes 33554432
  (44 shorter events, 30.5 us)
Async XLA Ops:
  0.6 52.3 %copy-start = (bf16[16,32,2048]{2,1,0:T(8,128)(2,1)S(1)}, bf16[16,32,2048]{2,1,0:T(8,128)(2,1)}, u32[]{:S(2)}) copy-start(bf16[16,32,2048]{2,1,0:T(8,128)(2,1)} %param.5) | copy-start | bytes 6291460
  3.8 47.3 %collective-permute-start = (bf16[15,32,2048]{2,1,0:T(8,128)(2,1)}, bf16[15,32,2048]{2,1,0:T(8,128)(2,1)}, u32[]{:S(2)}, u32[]{:S(2)}) collective-permute-start(bf16[15,32,2048]{2,1,0:T(8,128)(2,1)} %slice.112), channel_id=1, source_target_pairs={{0,1},{1,2},{2,3},{4,5},{5,6},{6,7},{8,9},{9,10},{10,11},{12,13},{... | collective-permute-start | bytes 5898248 | tf_op jit(solution)/shard_map/ppermute | solution.py:11
  203.8 53.3 %all-to-all-start.1 = ((bf16[1,128,256,2,16]{2,4,3,0,1:T(8,128)(2,1)}), bf16[1,128,256,2,16]{2,4,3,0,1:T(8,128)(2,1)S(1)}, u32[]{:S(2)}, u32[]{:S(2)}) async-start(bf16[1,128,256,2,16]{2,4,3,0,1:T(8,128)(2,1)} %copy.36), calls=%async_computation.1 | async-start | bytes 4194304 | tf_op jit(solution)/shard_map/all_to_all | solution.py:71
  258.4 111.2 %all-to-all-start.2 = ((f32[4,1,512]{2,1,0:T(1,128)}), f32[4,1,512]{2,1,0:T(1,128)S(1)}, u32[]{:S(2)}, u32[]{:S(2)}) async-start(f32[4,1,512]{2,1,0:T(1,128)} %reshape.84), calls=%async_computation.2 | async-start | bytes 16384 | tf_op jit(solution)/shard_map/all_to_all | solution.py:81
where the time goes:
time: 373 us; the launch traced here: 372 us
  other arithmetic  90.2 us (24%)
  waiting for transfers between devices  87 us (23%)
  matrix products  82.4 us (22%)
  local copies, waits for them, and re-layouts  65.6 us (18%)
  blocking collectives  30.2 us (8%)
  starting transfers between devices  15.2 us (4%)
    add x4, other arithmetic, accumulate(): return running + partial_value.astype(jnp.float32)  51.9 us
    all_to_all x1, waiting for transfers between devices, body(): lax.all_to_all(lax.all_to_all(spectra[None], 'station', split_axis=1, con...  47.5 us
    ppermute x1, waiting for transfers between devices, passed_along(): return lax.ppermute(block, axis, route)  39.5 us
    dot_general x1, matrix products, body(): jnp.einsum('nc,atn->cat', sin_part, weighted, preferred_element_type=jnp....  32.5 us
    dot_general x1, matrix products, body(): jnp.einsum('nc,atn->cat', cos_part, weighted, preferred_element_type=jnp....  31.8 us
    unnamed x7, local copies, waits for them, and re-layouts  31.2 us
    all_to_all x1, blocking collectives, body(): lax.all_to_all(spectra[None], 'station', split_axis=1, concat_axis=2, til...  30.2 us
    another operation x4, other arithmetic, accumulate(): jnp.stack([real_part, imag_part], axis=1).astype(jnp.bfloat16)  25.4 us
  transfers between devices with their start and end apart: 3, of which 2 were waited for; matrix products, arithmetic and copies ran while one was open for 29% of the time, Pallas kernels for 0%

commit v1 on v0

--- a/solution.py
+++ b/solution.py
@@ -3,6 +3,22 @@
 import jax.numpy as jnp
 from jax import lax
 from jax.sharding import PartitionSpec as P
+
+
+def pairwise_exchange(x, axis, split, join):
+    ways, here = (lax.axis_size(axis), lax.axis_index(axis))
+    width = x.shape[split] // ways
+    shape = list(x.shape)
+    shape[split] = width
+    height = shape[join]
+    shape[join] = height * ways
+    full = jnp.zeros(shape, x.dtype)
+    for mask in range(ways):
+        part = lax.dynamic_slice_in_dim(x, (here ^ mask) * width, width, axis=split)
+        if mask:
+            part = lax.ppermute(part, axis, [(d, d ^ mask) for d in range(ways)])
+        full = lax.dynamic_update_slice_in_dim(full, part, (here ^ mask) * height, axis=join)
+    return full
 
 
 def passed_along(block, axis, distance):
@@ -69,7 +85,7 @@
     time_groups = lax.axis_size("tm")
     norm_scale = 1.0 / (frames_dev * time_groups)
     gathered = lax.all_to_all(
-        lax.all_to_all(spectra[None], "station", split_axis=1, concat_axis=2, tiled=True),
+        pairwise_exchange(spectra[None], "station", 1, 2),
         "tm",
         split_axis=1,
         concat_axis=0,

time: 373 us -> 624 us (1.67); the launches traced: 372 us -> 615 us
  local copies, waits for them, and re-layouts: 65.6 us -> 328 us
  blocking collectives: 30.2 us -> 0 us
  starting transfers between devices: 15.2 us -> 22.7 us
    dynamic_update_slice x0 -> x8, local copies, waits for them, and re-layouts: none -> 289 us  [pairwise_exchange(): lax.dynamic_update_slice_in_dim(full, part, (here ^ mask) * height, axis=...]
    all_to_all x1 -> x0, blocking collectives: 30.2 us -> none  [body(): lax.all_to_all(spectra[None], 'station', split_axis=1, concat_axis=2, til...]
    unnamed x7 -> x5, local copies, waits for them, and re-layouts: 31.2 us -> 12.4 us
    all_to_all x3 -> x0, local copies, waits for them, and re-layouts: 15.9 us -> none  [body(): lax.all_to_all(spectra[None], 'station', split_axis=1, concat_axis=2, til...]
    ppermute x0 -> x7, local copies, waits for them, and re-layouts: none -> 13.4 us  [pairwise_exchange(): part = lax.ppermute(part, axis, [(d, d ^ mask) for d in range(ways)])]
    another operation x1 -> x7, local copies, waits for them, and re-layouts: 12.1 us -> 3.55 us  [body(): spectra = jnp.stack([real_spec, imag_spec], axis=2).astype(jnp.bfloat16)]
    ppermute x0 -> x7, starting transfers between devices: none -> 7.47 us  [pairwise_exchange(): part = lax.ppermute(part, axis, [(d, d ^ mask) for d in range(ways)])]
  transfers between devices with their start and end apart: 3 -> 10, of which waited for: 2 -> 3; matrix products, arithmetic and copies ran while one was open for 29% -> 61% of each run, Pallas kernels for 0% -> 0%
where the time goes in v1:
time: 624 us; the launch traced here: 615 us
  local copies, waits for them, and re-layouts  328 us (53%)
  other arithmetic  90.5 us (15%)
  waiting for transfers between devices  90.2 us (14%)
  matrix products  82.7 us (13%)
  starting transfers between devices  22.7 us (4%)
    dynamic_update_slice x8, local copies, waits for them, and re-layouts, pairwise_exchange(): lax.dynamic_update_slice_in_dim(full, part, (here ^ mask) * height, axis=...  289 us
    add x4, other arithmetic, accumulate(): return running + partial_value.astype(jnp.float32)  51.8 us
    all_to_all x1, waiting for transfers between devices, body(): lax.all_to_all(pairwise_exchange(spectra[None], 'station', 1, 2), 'tm', s...  49.5 us
    ppermute x1, waiting for transfers between devices, passed_along(): return lax.ppermute(block, axis, route)  39.5 us
    dot_general x1, matrix products, body(): jnp.einsum('nc,atn->cat', sin_part, weighted, preferred_element_type=jnp....  32.8 us
    dot_general x1, matrix products, body(): jnp.einsum('nc,atn->cat', cos_part, weighted, preferred_element_type=jnp....  31.8 us
    another operation x4, other arithmetic, accumulate(): jnp.stack([real_part, imag_part], axis=1).astype(jnp.bfloat16)  25.4 us
    ppermute x7, local copies, waits for them, and re-layouts, pairwise_exchange(): part = lax.ppermute(part, axis, [(d, d ^ mask) for d in range(ways)])  13.4 us
  transfers between devices with their start and end apart: 10, of which 3 were waited for; matrix products, arithmetic and copies ran while one was open for 61% of the time, Pallas kernels for 0%

profile of v1, /device:TPU:0, one launch (start us, length us, event | category | flops | bytes accessed | tf_op | source)
XLA Modules:
  0.0 615.0 jit_solution(16801796142537030364)
XLA Ops:
  3.8 6.2 %collective-permute-start = (bf16[15,32,2048]{2,1,0:T(8,128)(2,1)}, bf16[15,32,2048]{2,1,0:T(8,128)(2,1)}, u32[]{:S(2)}, u32[]{:S(2)}) collective-permute-start(bf16[15,32,2048]{2,1,0:T(8,128)(2,1)} %slice.112), channel_id=1, source_target_pairs={{0,1},{1,2},{2,3},{4,5},{5,6},{6,7},{8,9},{9,10},{10,11},{12,13},{... | collective-permute-start | bytes 5898248 | tf_op jit(solution)/shard_map/ppermute | solution.py:27
  11.7 39.5 %collective-permute-done = bf16[15,32,2048]{2,1,0:T(8,128)(2,1)} collective-permute-done((bf16[15,32,2048]{2,1,0:T(8,128)(2,1)}, bf16[15,32,2048]{2,1,0:T(8,128)(2,1)}, u32[]{:S(2)}, u32[]{:S(2)}) %collective-permute-start) | collective-permute-done | bytes 1966112 | tf_op jit(solution)/shard_map/ppermute | solution.py:27
  52.9 9.5 %add_convert_fusion = bf16[16,32,2048]{2,1,0:T(8,128)(2,1)S(1)} fusion(bf16[16,32,2048]{2,1,0:T(8,128)(2,1)S(1)} %copy-done, bf16[15,32,2048]{2,1,0:T(8,128)(2,1)S(1)} %broadcast_select_fusion, f32[2048]{0:T(1024)S(1)} %bitcast.133, f32[2048]{0:T(1024)S(1)} %bitcast.134, f32[2048]{0:T(1024)S(1)} %bitcast.120, f32[2048]{0:T(1024)S(1)} %bitcast.121, ...), kind=kLoop, calls=%fused_computation.53 | loop fusion | flops 66060288 | bytes 6291456 | tf_op jit(solution)/shard_map/convert_element_type | solution.py:46
  62.4 31.8 %fusion.42 = bf16[1024,32,1,16]{0,1,3,2:T(8,128)(2,1)S(1)} fusion(bf16[16,32,2048]{2,1,0:T(8,128)(2,1)S(1)} %add_convert_fusion), kind=kOutput, calls=%fused_computation.90 | convolution fusion | flops 2179465216 | bytes 3145728 | tf_op jit(solution)/shard_map/nc,atn->cat/dot_general | solution.py:82
  94.2 32.8 %fusion.47 = bf16[1024,32,1,16]{0,1,3,2:T(8,128)(2,1)S(1)} fusion(bf16[16,32,2048]{2,1,0:T(8,128)(2,1)S(1)} %add_convert_fusion), kind=kOutput, calls=%fused_computation.91 | convolution fusion | flops 2181562368 | bytes 3145728 | tf_op jit(solution)/shard_map/nc,atn->cat/dot_general | solution.py:83
  142.8 12.8 %dynamic_update_slice.24 = bf16[1,128,256,2,16]{2,4,3,0,1:T(8,128)(2,1)} dynamic-update-slice(bf16[1,128,256,2,16]{2,4,3,0,1:T(8,128)(2,1)} %broadcast_in_dim.10, bf16[1,128,32,2,16]{2,4,3,0,1:T(8,128)(2,1)S(1)} %copy.81, s32[]{:T(128)} %constant.65.clone.1, s32[]{:T(128)} %constant.65.clone.1, s32[]{:T(128)S(6)} %select_n.75, s32[]{:T(128)} %constant.65.clone.1, s32[]{:T(128)} %constant.65.clone.1) | dynamic-update-slice | bytes 524292 | tf_op jit(solution)/shard_map/dynamic_update_slice | solution.py:20
  157.2 44.3 %dynamic_update_slice.25 = bf16[1,128,256,2,16]{2,4,3,0,1:T(8,128)(2,1)} dynamic-update-slice(bf16[1,128,256,2,16]{2,4,3,0,1:T(8,128)(2,1)} %dynamic_update_slice.24, bf16[1,128,32,2,16]{2,4,3,0,1:T(8,128)(2,1)S(1)} %copy.83, s32[]{:T(128)} %constant.65.clone.1, s32[]{:T(128)} %constant.65.clone.1, s32[]{:T(128)S(6)} %select_n.77, s32[]{:T(128)} %constant.65.clone.1, s32[]{:T(128)} %constant.65.clone.1) | dynamic-update-slice | bytes 524292 | tf_op jit(solution)/shard_map/dynamic_update_slice | solution.py:20
  204.2 44.3 %dynamic_update_slice.26 = bf16[1,128,256,2,16]{2,4,3,0,1:T(8,128)(2,1)} dynamic-update-slice(bf16[1,128,256,2,16]{2,4,3,0,1:T(8,128)(2,1)} %dynamic_update_slice.25, bf16[1,128,32,2,16]{2,4,3,0,1:T(8,128)(2,1)S(1)} %copy.85, s32[]{:T(128)} %constant.65.clone.1, s32[]{:T(128)} %constant.65.clone.1, s32[]{:T(128)S(6)} %select_n.79, s32[]{:T(128)} %constant.65.clone.1, s32[]{:T(128)} %constant.65.clone.1) | dynamic-update-slice | bytes 524292 | tf_op jit(solution)/shard_map/dynamic_update_slice | solution.py:20
  251.2 44.3 %dynamic_update_slice.27 = bf16[1,128,256,2,16]{2,4,3,0,1:T(8,128)(2,1)} dynamic-update-slice(bf16[1,128,256,2,16]{2,4,3,0,1:T(8,128)(2,1)} %dynamic_update_slice.26, bf16[1,128,32,2,16]{2,4,3,0,1:T(8,128)(2,1)S(1)} %copy.87, s32[]{:T(128)} %constant.65.clone.1, s32[]{:T(128)} %constant.65.clone.1, s32[]{:T(128)S(6)} %select_n.81, s32[]{:T(128)} %constant.65.clone.1, s32[]{:T(128)} %constant.65.clone.1) | dynamic-update-slice | bytes 524292 | tf_op jit(solution)/shard_map/dynamic_update_slice | solution.py:20
  297.1 12.0 %dynamic_update_slice.28 = bf16[1,128,256,2,16]{2,4,3,0,1:T(8,128)(2,1)} dynamic-update-slice(bf16[1,128,256,2,16]{2,4,3,0,1:T(8,128)(2,1)} %dynamic_update_slice.27, bf16[1,128,32,2,16]{2,4,3,0,1:T(8,128)(2,1)S(1)} %copy.89, s32[]{:T(128)} %constant.65.clone.1, s32[]{:T(128)} %constant.65.clone.1, s32[]{:T(128)S(6)} %select_n.83, s32[]{:T(128)} %constant.65.clone.1, s32[]{:T(128)} %constant.65.clone.1) | dynamic-update-slice | bytes 524292 | tf_op jit(solution)/shard_map/dynamic_update_slice | solution.py:20
  310.7 43.9 %dynamic_update_slice.29 = bf16[1,128,256,2,16]{2,4,3,0,1:T(8,128)(2,1)} dynamic-update-slice(bf16[1,128,256,2,16]{2,4,3,0,1:T(8,128)(2,1)} %dynamic_update_slice.28, bf16[1,128,32,2,16]{2,4,3,0,1:T(8,128)(2,1)S(1)} %copy.91, s32[]{:T(128)} %constant.65.clone.1, s32[]{:T(128)} %constant.65.clone.1, s32[]{:T(128)S(6)} %select_n.85, s32[]{:T(128)} %constant.65.clone.1, s32[]{:T(128)} %constant.65.clone.1) | dynamic-update-slice | bytes 524292 | tf_op jit(solution)/shard_map/dynamic_update_slice | solution.py:20
  356.2 43.6 %dynamic_update_slice.30 = bf16[1,128,256,2,16]{2,4,3,0,1:T(8,128)(2,1)} dynamic-update-slice(bf16[1,128,256,2,16]{2,4,3,0,1:T(8,128)(2,1)} %dynamic_update_slice.29, bf16[1,128,32,2,16]{2,4,3,0,1:T(8,128)(2,1)S(1)} %copy.93, s32[]{:T(128)} %constant.65.clone.1, s32[]{:T(128)} %constant.65.clone.1, s32[]{:T(128)S(6)} %select_n.87, s32[]{:T(128)} %constant.65.clone.1, s32[]{:T(128)} %constant.65.clone.1) | dynamic-update-slice | bytes 524292 | tf_op jit(solution)/shard_map/dynamic_update_slice | solution.py:20
  401.5 43.6 %dynamic_update_slice.31 = bf16[1,128,256,2,16]{2,4,3,0,1:T(8,128)(2,1)} dynamic-update-slice(bf16[1,128,256,2,16]{2,4,3,0,1:T(8,128)(2,1)} %dynamic_update_slice.30, bf16[1,128,32,2,16]{2,4,3,0,1:T(8,128)(2,1)S(1)} %copy.95, s32[]{:T(128)} %constant.65.clone.1, s32[]{:T(128)} %constant.65.clone.1, s32[]{:T(128)S(6)} %select_n.89, s32[]{:T(128)} %constant.65.clone.1, s32[]{:T(128)} %constant.65.clone.1) | dynamic-update-slice | bytes 524292 | tf_op jit(solution)/shard_map/dynamic_update_slice | solution.py:20
  450.9 49.5 %all-to-all-done = bf16[1,128,256,2,16]{2,4,3,0,1:T(8,128)(2,1)S(1)} async-done(((bf16[1,128,256,2,16]{2,4,3,0,1:T(8,128)(2,1)}), bf16[1,128,256,2,16]{2,4,3,0,1:T(8,128)(2,1)S(1)}, u32[]{:S(2)}, u32[]{:S(2)}) %all-to-all-start) | async-done | bytes 2097184 | tf_op jit(solution)/shard_map/all_to_all | solution.py:87
  505.0 96.2 %while.14 = (s32[]{:T(128)}, f32[32,2,256,256]{3,2,0,1:T(8,128)}, bf16[4,32,256,2,16]{2,4,3,1,0:T(8,128)(2,1)S(1)}, s32[]{:T(128)}, s32[]{:T(128)}) while((s32[]{:T(128)}, f32[32,2,256,256]{3,2,0,1:T(8,128)}, bf16[4,32,256,2,16]{2,4,3,1,0:T(8,128)(2,1)S(1)}, s32[]{:T(128)}, s32[]{:T(128)}) %tuple.69), condition=%wide.region_1.2_spmd.clone, body=%wide.region_0.1_spmd.clone.sunk | while | flops 293994496 | bytes 72876112 | solution.py:108
  509.8 6.3 %pad_maximum_fusion.6 = bf16[32,2,256,256]{3,2,0,1:T(8,128)(2,1)} fusion(bf16[32,1,256,256]{3,2,0,1:T(8,128)(2,1)S(1)} %fusion.87, bf16[32,1,256,256]{3,2,0,1:T(8,128)(2,1)} %fusion.88), kind=kLoop, calls=%fused_computation.1.clone.1 | loop fusion | flops 4194304 | bytes 16777216 | tf_op jit(solution)/shard_map/while/body/eval_jaxpr/stack | solution.py:103
  516.1 9.9 %select_add_fusion.2 = f32[32,2,256,256]{3,2,0,1:T(8,128)} fusion(f32[32,2,256,256]{3,2,0,1:T(8,128)} %get-tuple-element.152, bf16[32,2,256,256]{3,2,0,1:T(8,128)(2,1)} %pad_maximum_fusion.6, pred[]{:T(512)S(6)} %compare.4), kind=kLoop, calls=%fused_computation.clone.1 | loop fusion | flops 12582912 | bytes 41943040 | tf_op jit(solution)/shard_map/while/body/eval_jaxpr/add | solution.py:105
  530.8 6.3 %pad_maximum_fusion.6 = bf16[32,2,256,256]{3,2,0,1:T(8,128)(2,1)} fusion(bf16[32,1,256,256]{3,2,0,1:T(8,128)(2,1)S(1)} %fusion.87, bf16[32,1,256,256]{3,2,0,1:T(8,128)(2,1)} %fusion.88), kind=kLoop, calls=%fused_computation.1.clone.1 | loop fusion | flops 4194304 | bytes 16777216 | tf_op jit(solution)/shard_map/while/body/eval_jaxpr/stack | solution.py:103
  537.1 14.0 %select_add_fusion.2 = f32[32,2,256,256]{3,2,0,1:T(8,128)} fusion(f32[32,2,256,256]{3,2,0,1:T(8,128)} %get-tuple-element.152, bf16[32,2,256,256]{3,2,0,1:T(8,128)(2,1)} %pad_maximum_fusion.6, pred[]{:T(512)S(6)} %compare.4), kind=kLoop, calls=%fused_computation.clone.1 | loop fusion | flops 12582912 | bytes 41943040 | tf_op jit(solution)/shard_map/while/body/eval_jaxpr/add | solution.py:105
  555.8 6.3 %pad_maximum_fusion.6 = bf16[32,2,256,256]{3,2,0,1:T(8,128)(2,1)} fusion(bf16[32,1,256,256]{3,2,0,1:T(8,128)(2,1)S(1)} %fusion.87, bf16[32,1,256,256]{3,2,0,1:T(8,128)(2,1)} %fusion.88), kind=kLoop, calls=%fused_computation.1.clone.1 | loop fusion | flops 4194304 | bytes 16777216 | tf_op jit(solution)/shard_map/while/body/eval_jaxpr/stack | solution.py:103
  562.2 14.0 %select_add_fusion.2 = f32[32,2,256,256]{3,2,0,1:T(8,128)} fusion(f32[32,2,256,256]{3,2,0,1:T(8,128)} %get-tuple-element.152, bf16[32,2,256,256]{3,2,0,1:T(8,128)(2,1)} %pad_maximum_fusion.6, pred[]{:T(512)S(6)} %compare.4), kind=kLoop, calls=%fused_computation.clone.1 | loop fusion | flops 12582912 | bytes 41943040 | tf_op jit(solution)/shard_map/while/body/eval_jaxpr/add | solution.py:105
  580.9 6.3 %pad_maximum_fusion.6 = bf16[32,2,256,256]{3,2,0,1:T(8,128)(2,1)} fusion(bf16[32,1,256,256]{3,2,0,1:T(8,128)(2,1)S(1)} %fusion.87, bf16[32,1,256,256]{3,2,0,1:T(8,128)(2,1)} %fusion.88), kind=kLoop, calls=%fused_computation.1.clone.1 | loop fusion | flops 4194304 | bytes 16777216 | tf_op jit(solution)/shard_map/while/body/eval_jaxpr/stack | solution.py:103
  587.2 14.0 %select_add_fusion.2 = f32[32,2,256,256]{3,2,0,1:T(8,128)} fusion(f32[32,2,256,256]{3,2,0,1:T(8,128)} %get-tuple-element.152, bf16[32,2,256,256]{3,2,0,1:T(8,128)(2,1)} %pad_maximum_fusion.6, pred[]{:T(512)S(6)} %compare.4), kind=kLoop, calls=%fused_computation.clone.1 | loop fusion | flops 12582912 | bytes 41943040 | tf_op jit(solution)/shard_map/while/body/eval_jaxpr/add | solution.py:105
  601.2 11.7 %copy.99 = f32[32,2,256,256]{3,2,1,0:T(8,128)} copy(f32[32,2,256,256]{3,2,0,1:T(8,128)} %get-tuple-element.89) | data formatting | bytes 33554432
  (76 shorter events, 67.0 us)
Async XLA Ops:
  0.6 52.3 %copy-start = (bf16[16,32,2048]{2,1,0:T(8,128)(2,1)S(1)}, bf16[16,32,2048]{2,1,0:T(8,128)(2,1)}, u32[]{:S(2)}) copy-start(bf16[16,32,2048]{2,1,0:T(8,128)(2,1)} %param.5) | copy-start | bytes 6291460
  3.8 47.3 %collective-permute-start = (bf16[15,32,2048]{2,1,0:T(8,128)(2,1)}, bf16[15,32,2048]{2,1,0:T(8,128)(2,1)}, u32[]{:S(2)}, u32[]{:S(2)}) collective-permute-start(bf16[15,32,2048]{2,1,0:T(8,128)(2,1)} %slice.112), channel_id=1, source_target_pairs={{0,1},{1,2},{2,3},{4,5},{5,6},{6,7},{8,9},{9,10},{10,11},{12,13},{... | collective-permute-start | bytes 5898248 | tf_op jit(solution)/shard_map/ppermute | solution.py:27
  128.2 6.5 %collective-permute-start.1 = (bf16[1,128,32,2,16]{1,4,3,2,0:T(8,128)(2,1)}, bf16[1,128,32,2,16]{1,4,3,2,0:T(8,128)(2,1)S(1)}, u32[]{:S(2)}, u32[]{:S(2)}) collective-permute-start(bf16[1,128,32,2,16]{1,4,3,2,0:T(8,128)(2,1)} %bitcast.90), channel_id=1, source_target_pairs={{0,4},{4,0},{8,12},{12,8},{16,20},{20,16},{24,28},{28,24},{1,5},{5... | collective-permute-start | bytes 786440 | tf_op jit(solution)/shard_map/ppermute | solution.py:19
  129.0 9.4 %collective-permute-start.2 = (bf16[1,128,32,2,16]{1,4,3,2,0:T(8,128)(2,1)}, bf16[1,128,32,2,16]{1,4,3,2,0:T(8,128)(2,1)}, u32[]{:S(2)}, u32[]{:S(2)}) collective-permute-start(bf16[1,128,32,2,16]{1,4,3,2,0:T(8,128)(2,1)} %bitcast.89), channel_id=1, source_target_pairs={{0,8},{4,12},{8,0},{12,4},{16,24},{20,28},{24,16},{28,20},{1,9},{5... | collective-permute-start | bytes 786440 | tf_op jit(solution)/shard_map/ppermute | solution.py:19
  131.3 117.2 %collective-permute-start.3 = (bf16[1,128,32,2,16]{1,4,3,2,0:T(8,128)(2,1)}, bf16[1,128,32,2,16]{1,4,3,2,0:T(8,128)(2,1)}, u32[]{:S(2)}, u32[]{:S(2)}) collective-permute-start(bf16[1,128,32,2,16]{1,4,3,2,0:T(8,128)(2,1)} %bitcast.88), channel_id=1, source_target_pairs={{0,12},{4,8},{8,4},{12,0},{16,28},{20,24},{24,20},{28,16},{1,13},{... | collective-permute-start | bytes 786440 | tf_op jit(solution)/shard_map/ppermute | solution.py:19
  132.5 163.0 %collective-permute-start.4 = (bf16[1,128,32,2,16]{1,4,3,2,0:T(8,128)(2,1)}, bf16[1,128,32,2,16]{1,4,3,2,0:T(8,128)(2,1)S(1)}, u32[]{:S(2)}, u32[]{:S(2)}) collective-permute-start(bf16[1,128,32,2,16]{1,4,3,2,0:T(8,128)(2,1)} %bitcast.87), channel_id=1, source_target_pairs={{0,16},{4,20},{8,24},{12,28},{16,0},{20,4},{24,8},{28,12},{1,17},{... | collective-permute-start | bytes 786440 | tf_op jit(solution)/shard_map/ppermute | solution.py:19
  134.2 174.9 %collective-permute-start.5 = (bf16[1,128,32,2,16]{1,4,3,2,0:T(8,128)(2,1)S(1)}, bf16[1,128,32,2,16]{1,4,3,2,0:T(8,128)(2,1)S(1)}, u32[]{:S(2)}, u32[]{:S(2)}) collective-permute-start(bf16[1,128,32,2,16]{1,4,3,2,0:T(8,128)(2,1)S(1)} %bitcast.116), channel_id=1, source_target_pairs={{0,20},{4,16},{8,28},{12,24},{16,4},{20,0},{24,12},{28,8},{1,21},{... | collective-permute-start | bytes 786440 | tf_op jit(solution)/shard_map/ppermute | solution.py:19
  134.6 219.9 %collective-permute-start.6 = (bf16[1,128,32,2,16]{1,4,3,2,0:T(8,128)(2,1)S(1)}, bf16[1,128,32,2,16]{1,4,3,2,0:T(8,128)(2,1)S(1)}, u32[]{:S(2)}, u32[]{:S(2)}) collective-permute-start(bf16[1,128,32,2,16]{1,4,3,2,0:T(8,128)(2,1)S(1)} %bitcast.115), channel_id=1, source_target_pairs={{0,24},{4,28},{8,16},{12,20},{16,8},{20,12},{24,0},{28,4},{1,25},{... | collective-permute-start | bytes 786440 | tf_op jit(solution)/shard_map/ppermute | solution.py:19
  138.4 261.4 %collective-permute-start.7 = (bf16[1,128,32,2,16]{1,4,3,2,0:T(8,128)(2,1)S(1)}, bf16[1,128,32,2,16]{1,4,3,2,0:T(8,128)(2,1)S(1)}, u32[]{:S(2)}, u32[]{:S(2)}) collective-permute-start(bf16[1,128,32,2,16]{1,4,3,2,0:T(8,128)(2,1)S(1)} %bitcast.114), channel_id=1, source_target_pairs={{0,28},{4,24},{8,20},{12,16},{16,12},{20,8},{24,4},{28,0},{1,29},{... | collective-permute-start | bytes 786440 | tf_op jit(solution)/shard_map/ppermute | solution.py:19
  445.1 55.3 %all-to-all-start = ((bf16[1,128,256,2,16]{2,4,3,0,1:T(8,128)(2,1)}), bf16[1,128,256,2,16]{2,4,3,0,1:T(8,128)(2,1)S(1)}, u32[]{:S(2)}, u32[]{:S(2)}) async-start(bf16[1,128,256,2,16]{2,4,3,0,1:T(8,128)(2,1)} %dynamic_update_slice.31), calls=%async_computation | async-start | bytes 4194304 | tf_op jit(solution)/shard_map/all_to_all | solution.py:87
  501.7 111.1 %all-to-all-start.1 = ((f32[4,1,512]{2,1,0:T(1,128)}), f32[4,1,512]{2,1,0:T(1,128)S(1)}, u32[]{:S(2)}, u32[]{:S(2)}) async-start(f32[4,1,512]{2,1,0:T(1,128)} %reshape.57), calls=%async_computation.1 | async-start | bytes 16384 | tf_op jit(solution)/shard_map/all_to_all | solution.py:97
